TPU v7x, 128 devices: a whole 4x4x4 slice. The times are simulated.
128 devices in a mesh: ang: 16 (over z_lo, x, core), kslab: 8 (over z_hi, y).
Axes of the slice: x: 4, y: 4, z: 4 (z_hi: 2, z_lo: 2; z = z_hi * 2 + z_lo), core: 2. Of those that a mesh axis runs over, the one named last changes fastest.
Arguments:
- amplitude: bfloat16 [256, 112, 8, 2048], P('ang', None, 'kslab'), may hold values from -6 to 6
- ps_form: bfloat16 [2048, 896], replicated, may hold values from -0.125 to 0.125
- kgrid: float32 [8], replicated, may hold values from 0.1 to 3
- l_atom: int32 [112], replicated, may hold values from 0 to 7
- l_ps: int32 [112], replicated, may hold values from 0 to 7
- sixj: float32 [8, 12, 8, 8], replicated, may hold values from -0.5 to 0.5
Outputs:
- kernel: float32 [112, 8, 8, 896], P('ang', 'kslab')
All inputs are finite; a program needn't handle non-finite values.
Results may differ from a plain program's by a relative error of at most 0.0003.
Values sent between devices are 32-bit elements; how exact they have to be, the bound alone decides.
No kernel may reach another device: no remote copies, remote signals or barrier semaphores. Data moves between devices by JAX's collectives and lax.ppermute only.
A program may use at most 128 MiB of HBM per device.

v0:
```python
import jax
import jax.numpy as jnp
from jax import lax
from jax.sharding import PartitionSpec as P


def legendre_table(first_row, row_count, total_points, degrees):
    positions = (first_row + jnp.arange(row_count)).astype(jnp.float32)
    angles = jnp.pi * (positions + 0.5) / total_points
    grid_nodes = jnp.cos(angles)
    grid_weights = jnp.pi / total_points * jnp.sin(angles)
    series = [jnp.ones_like(grid_nodes), grid_nodes]
    for degree in range(1, degrees - 1):
        series.append(
            ((2 * degree + 1) * grid_nodes * series[-1] - degree * series[-2]) / (degree + 1)
        )
    return (grid_nodes, grid_weights[None, :] * jnp.stack(series[:degrees]))


def recouple(values, channel_first, j_first, j_count, l_atom, l_ps, sixj, kpoints):
    channel_count = values.shape[0]
    levels = jnp.arange(sixj.shape[2], dtype=jnp.int32)
    atom_levels = lax.dynamic_slice_in_dim(l_atom, channel_first, channel_count)
    onehot_atom = (atom_levels[:, None] == levels[None, :]).astype(jnp.float32)
    onehot_ps = (l_ps[:, None] == levels[None, :]).astype(jnp.float32)
    table = lax.dynamic_slice_in_dim(sixj, j_first, j_count, 0)
    coupling = jnp.einsum(
        "jlxy,ax,by->ajlb", table, onehot_atom, onehot_ps, precision=lax.Precision.HIGHEST
    )
    widened = jnp.repeat(coupling, kpoints, axis=3)
    return jnp.einsum("ajlc,alkc->ajkc", widened, values, precision=lax.Precision.HIGHEST)


def local(amplitude, ps_form, kgrid, l_atom, l_ps, sixj):
    grid_count, channels, slab_points, radial = amplitude.shape
    columns = ps_form.shape[1]
    kpoints = kgrid.shape[0]
    ps_channels = columns // kpoints
    degrees = sixj.shape[1]
    total_j = sixj.shape[0]
    ang_size = lax.axis_size("ang")
    slab_size = lax.axis_size("kslab")
    owned = channels // ang_size
    owned_first = lax.axis_index("ang") * owned
    j_local = total_j // slab_size
    j_first = lax.axis_index("kslab") * j_local
    grid_nodes, projector = legendre_table(
        lax.axis_index("ang") * grid_count, grid_count, grid_count * ang_size, degrees
    )
    krow = lax.dynamic_slice_in_dim(kgrid, lax.axis_index("kslab") * slab_points, slab_points)[
        None, :, None
    ]
    kcol = jnp.tile(kgrid, ps_channels)[None, None, :]
    qinverse = 1.0 / (
        1.0 + krow * krow + kcol * kcol - 2.0 * grid_nodes[:, None, None] * krow * kcol
    )
    intersection = jnp.dot(
        amplitude.reshape(-1, radial), ps_form, preferred_element_type=jnp.float32
    )
    intersection = intersection.reshape(
        grid_count, lax.axis_size("ang") * owned, slab_points, columns
    )
    integrand = intersection * qinverse[:, None]
    summed = lax.psum_scatter(
        jnp.einsum("lg,gakc->alkc", projector, integrand, precision=lax.Precision.HIGHEST),
        "ang",
        scatter_dimension=0,
        tiled=True,
    )
    return recouple(
        lax.all_gather(summed, "kslab", axis=2, tiled=True),
        owned_first,
        j_first,
        j_local,
        l_atom,
        l_ps,
        sixj,
        kpoints,
    )


def solution(mesh):
    in_specs = (P("ang", None, "kslab", None), P(), P(), P(), P(), P())
    out_specs = P("ang", "kslab", None, None)
    return jax.shard_map(local, mesh=mesh, in_specs=in_specs, out_specs=out_specs, check_vma=False)
```

profile of v0, /device:TPU:1, one launch (start us, length us, event | category | flops | bytes accessed | tf_op | source)
XLA Modules:
  0.0 186.4 jit_solution(9028260817376288900)
XLA Ops:
  6.5 0.0 copy-start
  6.5 0.0 reduce-scatter.2.cloned.1.call-start
  6.5 0.1 broadcast_multiply_fusion.1
  6.6 0.1 broadcast_multiply_fusion.3
  6.7 0.1 broadcast_multiply_fusion.5
  6.7 0.1 subtract_multiply_fusion
  6.8 0.1 multiply_cosine_fusion
  6.9 0.1 broadcast_multiply_fusion.7
  6.9 1.2 dynamic_slice.9
  10.2 0.7 tile.2
  10.8 0.1 broadcast_in_dim_tile.3
  11.0 0.1 subtract_divide_fusion
  11.0 21.4 %fusion = f32[16,112,896]{2,0,1:T(8,128)} fusion(bf16[16,112,2048]{2,1,0:T(8,128)(2,1)} %bitcast.36, bf16[2048,896]{1,0:T(8,128)(2,1)} %param.7), kind=kOutput, calls=%fused_computation | convolution fusion | flops 6576668672 | bytes 17432576 | tf_op jit(solution)/shard_map/dot_general | solution.py:57
  32.5 0.1 stack.2
  32.5 9.5 %fusion.6 = f32[112,12,1,896]{3,1,0,2:T(8,128)} fusion(f32[16,112,896]{2,0,1:T(8,128)} %fusion, f32[16,896]{1,0:T(8,128)S(1)} %subtract_divide_fusion, f32[12,16]{1,0:T(8,128)S(1)} %stack.2, f32[16]{0:T(128)S(1)} %get-tuple-element.9), kind=kOutput, calls=%fused_computation.7 | convolution fusion | flops 232816832 | bytes 11297600 | tf_op jit(solution)/shard_map/lg,gakc->alkc/dot_general | solution.py:65
  42.0 0.0 reduce-scatter.2.cloned.1.call-update
  42.1 0.2 all-gather.2.cloned.1.call-start
  42.3 70.3 %reduce-scatter.2.cloned.1.call-done = f32[7,12,1,896]{3,1,0,2:T(8,128)} async-done(((f32[112,12,1,896]{3,1,0,2:T(8,128)}), f32[7,12,1,896]{3,1,0,2:T(8,128)}) %reduce-scatter.2.cloned.1.call-update) | async-done | bytes 301072 | tf_op jit(solution)/shard_map/reduce_scatter | solution.py:64
  112.6 1.8 copy.9
  114.4 0.0 all-gather.2.cloned.1.call-update
  114.4 0.0 copy-done.2
  114.4 0.1 dynamic_slice.10
  114.5 0.0 copy-done
  114.5 0.2 fusion.9
  114.7 0.1 copy.13
  114.9 0.0 copy-done.1
  114.9 0.2 fusion.18
  115.1 3.3 %broadcast_in_dim.4 = f32[7,12,112,8]{3,2,0,1:T(8,128)} broadcast(f32[7,12,112]{2,0,1:T(8,128)S(1)} %fusion.18), dimensions={0,1,2} | broadcast | bytes 338688 | tf_op jit(solution)/shard_map/broadcast_in_dim | solution.py:30
  118.4 4.1 %broadcast_in_dim.5 = f32[7,12,896]{2,0,1:T(8,128)S(1)} reshape(f32[7,12,112,8]{3,2,0,1:T(8,128)} %broadcast_in_dim.4) | data formatting | bytes 602112 | tf_op jit(solution)/shard_map/broadcast_in_dim | solution.py:30
  122.4 54.3 %all-gather.2.cloned.1.call-done = f32[7,12,8,896]{3,0,1,2:T(8,128)} async-done(((f32[7,12,1,896]{3,0,1,2:T(8,128)}), f32[7,12,8,896]{3,0,1,2:T(8,128)}) %all-gather.2.cloned.1.call-update) | async-done | bytes 2408464 | tf_op jit(solution)/shard_map/all_gather | solution.py:71
  176.7 2.1 %multiply_reduce_fusion = f32[7,896,8]{1,0,2:T(8,128)S(1)} fusion(f32[7,12,8,896]{3,0,1,2:T(8,128)} %all-gather.2.cloned.1.call-done, f32[7,896,12]{1,0,2:T(8,128)S(1)} %bitcast.35), kind=kLoop, calls=%fused_computation.6 | loop fusion | flops 1154048 | bytes 2910208
  178.8 0.7 copy.32
  (6 shorter events, 0.1 us)
Async XLA Ops:
  6.5 108.0 %copy-start = (f32[8,12,8,8]{1,3,2,0:T(8,128)S(1)}, f32[8,12,8,8]{1,3,2,0:T(8,128)}, u32[]{:S(2)}) copy-start(f32[8,12,8,8]{1,3,2,0:T(8,128)} %param.11) | copy-start | bytes 73732
  6.5 106.0 %reduce-scatter.2.cloned.1.call-start = ((), (), s32[]{:S(2)}) async-start(), calls=%async_computation.1 | async-start | bytes 6823936 | tf_op jit(solution)/shard_map/reduce_scatter | solution.py:64
  42.0 72.4 %copy-start.2 = (s32[112]{0:T(128)S(1)}, s32[112]{0:T(128)}, u32[]{:S(2)}) copy-start(s32[112]{0:T(128)} %param.9) | copy-start | bytes 1348
  42.0 72.8 %copy-start.1 = (s32[112]{0:T(128)S(1)}, s32[112]{0:T(128)}, u32[]{:S(2)}) copy-start(s32[112]{0:T(128)} %param.10) | copy-start | bytes 1348
  42.1 134.7 %all-gather.2.cloned.1.call-start = ((), (), s32[]{:S(2)}) async-start(), calls=%async_computation.2 | async-start | bytes 3096576 | tf_op jit(solution)/shard_map/all_gather | solution.py:71
Sparse Core Ops, SparseCore 0:
  42.2 70.3 reduce-scatter.1
  114.9 61.8 all-gather.1
where the time goes:
time: 187 us; the launch traced here: 186 us
  waiting for transfers between devices  125 us (67%)
  matrix products  31.3 us (17%)
  between operations  15.4 us (8%)
  local copies, waits for them, and re-layouts  12.2 us (7%)
  other arithmetic  2.6 us (1%)
    reduce_scatter x1, waiting for transfers between devices, local(): lax.psum_scatter(jnp.einsum('lg,gakc->alkc', projector, integrand, precis...  70.3 us
    all_gather x1, waiting for transfers between devices, local(): lax.all_gather(summed, 'kslab', axis=2, tiled=True)  54.3 us
    dot_general x1, matrix products, local(): jnp.dot(amplitude.reshape(-1, radial), ps_form, preferred_element_type=jn...  21.4 us
    dot_general x1, matrix products, local(): jnp.einsum('lg,gakc->alkc', projector, integrand, precision=lax.Precision...  9.49 us
    broadcast_in_dim x2, local copies, waits for them, and re-layouts, recouple(): widened = jnp.repeat(coupling, kpoints, axis=3)  7.37 us
  transfers between devices with their start and end apart: 2, of which 2 were waited for; matrix products, arithmetic and copies ran while one was open for 4% of the time, Pallas kernels for 0%

commit v1 on v0

--- a/solution.py
+++ b/solution.py
@@ -68,7 +68,9 @@
         tiled=True,
     )
     return recouple(
-        lax.all_gather(summed, "kslab", axis=2, tiled=True),
+        jnp.concatenate(
+            lax.all_to_all(jnp.stack([summed] * lax.axis_size("kslab")), "kslab", 0, 0), axis=2
+        ),
         owned_first,
         j_first,
         j_local,

time: 187 us -> 166 us (0.89); the launches traced: 186 us -> 162 us
  waiting for transfers between devices: 125 us -> 94.4 us
  starting transfers between devices: 0.22 us -> 6.46 us
    all_gather x1 -> x0, waiting for transfers between devices: 54.3 us -> none  [local(): lax.all_gather(summed, 'kslab', axis=2, tiled=True)]
    all_to_all x0 -> x1, waiting for transfers between devices: none -> 23.8 us  [local(): lax.all_to_all(jnp.stack([summed] * lax.axis_size('kslab')), 'kslab', 0, 0)]
    all_to_all x0 -> x1, starting transfers between devices: none -> 6.46 us  [local(): lax.all_to_all(jnp.stack([summed] * lax.axis_size('kslab')), 'kslab', 0, 0)]
    another operation x1 -> x2, local copies, waits for them, and re-layouts: 0.01 us -> 3.7 us  [the longest x1 3.7 us: local(): jnp.stack([summed] * lax.axis_size('kslab'))]
    unnamed x1 -> x0, other arithmetic: 2.07 us -> none
  transfers between devices with their start and end apart: 2 -> 2, of which waited for: 2 -> 2; matrix products, arithmetic and copies ran while one was open for 4% -> 5% of each run, Pallas kernels for 0% -> 0%
where the time goes in v1:
time: 166 us; the launch traced here: 162 us
  waiting for transfers between devices  94.4 us (57%)
  matrix products  31.3 us (19%)
  between operations  15.4 us (9%)
  local copies, waits for them, and re-layouts  13.4 us (8%)
  starting transfers between devices  6.46 us (4%)
    reduce_scatter x1, waiting for transfers between devices, local(): lax.psum_scatter(jnp.einsum('lg,gakc->alkc', projector, integrand, precis...  70.5 us
    all_to_all x1, waiting for transfers between devices, local(): lax.all_to_all(jnp.stack([summed] * lax.axis_size('kslab')), 'kslab', 0, 0)  23.8 us
    dot_general x1, matrix products, local(): jnp.dot(amplitude.reshape(-1, radial), ps_form, preferred_element_type=jn...  21.4 us
    dot_general x1, matrix products, local(): jnp.einsum('lg,gakc->alkc', projector, integrand, precision=lax.Precision...  9.49 us
    broadcast_in_dim x2, local copies, waits for them, and re-layouts, recouple(): widened = jnp.repeat(coupling, kpoints, axis=3)  7.37 us
    all_to_all x1, starting transfers between devices, local(): lax.all_to_all(jnp.stack([summed] * lax.axis_size('kslab')), 'kslab', 0, 0)  6.46 us
    another operation x1, local copies, waits for them, and re-layouts, local(): jnp.stack([summed] * lax.axis_size('kslab'))  3.7 us
  transfers between devices with their start and end apart: 2, of which 2 were waited for; matrix products, arithmetic and copies ran while one was open for 5% of the time, Pallas kernels for 0%

profile of v1, /device:TPU:1, one launch (start us, length us, event | category | flops | bytes accessed | tf_op | source)
XLA Modules:
  0.0 162.4 jit_solution(9469897989775629981)
XLA Ops:
  6.5 0.0 copy-start
  6.5 0.0 reduce-scatter.2.cloned.1.call-start
  6.5 0.1 broadcast_multiply_fusion.1
  6.6 0.1 broadcast_multiply_fusion.3
  6.7 0.1 broadcast_multiply_fusion.5
  6.7 0.1 subtract_multiply_fusion
  6.8 0.1 multiply_cosine_fusion
  6.9 0.1 broadcast_multiply_fusion.7
  6.9 1.2 dynamic_slice.9
  10.2 0.7 tile.2
  10.8 0.1 broadcast_in_dim_tile.3
  11.0 0.1 subtract_divide_fusion
  11.0 21.4 %fusion = f32[16,112,896]{2,0,1:T(8,128)} fusion(bf16[16,112,2048]{2,1,0:T(8,128)(2,1)} %bitcast.43, bf16[2048,896]{1,0:T(8,128)(2,1)} %param.7), kind=kOutput, calls=%fused_computation | convolution fusion | flops 6576668672 | bytes 17432576 | tf_op jit(solution)/shard_map/dot_general | solution.py:57
  32.5 0.1 stack.4
  32.5 9.5 %fusion.6 = f32[112,12,1,896]{3,1,0,2:T(8,128)} fusion(f32[16,112,896]{2,0,1:T(8,128)} %fusion, f32[16,896]{1,0:T(8,128)S(1)} %subtract_divide_fusion, f32[12,16]{1,0:T(8,128)S(1)} %stack.4, f32[16]{0:T(128)S(1)} %get-tuple-element.9), kind=kOutput, calls=%fused_computation.6 | convolution fusion | flops 232816832 | bytes 11297600 | tf_op jit(solution)/shard_map/lg,gakc->alkc/dot_general | solution.py:65
  42.0 0.0 copy-start.2
  42.0 0.0 reduce-scatter.2.cloned.1.call-update
  42.1 70.5 %reduce-scatter.2.cloned.1.call-done = f32[7,12,1,896]{3,1,0,2:T(8,128)} async-done(((f32[112,12,1,896]{3,1,0,2:T(8,128)}), f32[7,12,1,896]{3,1,0,2:T(8,128)}) %reduce-scatter.2.cloned.1.call-update) | async-done | bytes 301072 | tf_op jit(solution)/shard_map/reduce_scatter | solution.py:64
  112.6 3.7 %stack.5 = f32[8,7,12,1,896]{4,3,2,1,0:T(1,128)} broadcast(f32[7,12,896]{2,1,0:T(8,128)} %bitcast.42), dimensions={1,2,4} | broadcast | bytes 2709504 | tf_op jit(solution)/shard_map/stack | solution.py:72
  116.3 6.5 %all-to-all-start = ((f32[8,7,12,1,896]{4,3,2,1,0:T(1,128)}), f32[8,7,12,1,896]{4,3,2,1,0:T(1,128)S(1)}, u32[]{:S(2)}, u32[]{:S(2)}) async-start(f32[8,7,12,1,896]{4,3,2,1,0:T(1,128)} %stack.5), calls=%async_computation.1 | async-start | bytes 4816896 | tf_op jit(solution)/shard_map/all_to_all | solution.py:72
  122.8 0.0 copy-done.2
  122.8 0.1 dynamic_slice.10
  122.8 0.0 copy-done
  122.8 0.2 fusion.10
  123.0 0.1 copy.18
  123.2 0.0 copy-done.1
  123.2 0.2 fusion.19
  123.4 3.3 %broadcast_in_dim.4 = f32[7,12,112,8]{3,2,0,1:T(8,128)} broadcast(f32[7,12,112]{2,0,1:T(8,128)S(1)} %fusion.19), dimensions={0,1,2} | broadcast | bytes 338688 | tf_op jit(solution)/shard_map/broadcast_in_dim | solution.py:30
  126.7 4.1 %broadcast_in_dim.5 = f32[7,12,896]{2,0,1:T(8,128)S(1)} reshape(f32[7,12,112,8]{3,2,0,1:T(8,128)} %broadcast_in_dim.4) | data formatting | bytes 602112 | tf_op jit(solution)/shard_map/broadcast_in_dim | solution.py:30
  130.8 0.1 copy.29
  130.8 23.8 %all-to-all-done = f32[8,7,12,1,896]{4,3,2,1,0:T(1,128)S(1)} async-done(((f32[8,7,12,1,896]{4,3,2,1,0:T(1,128)}), f32[8,7,12,1,896]{4,3,2,1,0:T(1,128)S(1)}, u32[]{:S(2)}, u32[]{:S(2)}) %all-to-all-start) | async-done | bytes 2408480 | tf_op jit(solution)/shard_map/all_to_all | solution.py:72
  154.6 0.9 fusion.9
  (5 shorter events, 0.1 us)
Async XLA Ops:
  6.5 116.3 %copy-start = (f32[8,12,8,8]{1,3,2,0:T(8,128)S(1)}, f32[8,12,8,8]{1,3,2,0:T(8,128)}, u32[]{:S(2)}) copy-start(f32[8,12,8,8]{1,3,2,0:T(8,128)} %param.11) | copy-start | bytes 73732
  6.5 106.1 %reduce-scatter.2.cloned.1.call-start = ((), (), s32[]{:S(2)}) async-start(), calls=%async_computation.2 | async-start | bytes 6823936 | tf_op jit(solution)/shard_map/reduce_scatter | solution.py:64
  42.0 80.7 %copy-start.2 = (s32[112]{0:T(128)S(1)}, s32[112]{0:T(128)}, u32[]{:S(2)}) copy-start(s32[112]{0:T(128)} %param.9) | copy-start | bytes 1348
  42.0 81.1 %copy-start.1 = (s32[112]{0:T(128)S(1)}, s32[112]{0:T(128)}, u32[]{:S(2)}) copy-start(s32[112]{0:T(128)} %param.10) | copy-start | bytes 1348
  116.3 38.3 %all-to-all-start = ((f32[8,7,12,1,896]{4,3,2,1,0:T(1,128)}), f32[8,7,12,1,896]{4,3,2,1,0:T(1,128)S(1)}, u32[]{:S(2)}, u32[]{:S(2)}) async-start(f32[8,7,12,1,896]{4,3,2,1,0:T(1,128)} %stack.5), calls=%async_computation.1 | async-start | bytes 4816896 | tf_op jit(solution)/shard_map/all_to_all | solution.py:72
Sparse Core Ops, SparseCore 0:
  42.2 70.3 reduce-scatter.1
